TPU v7x, 32 devices: a whole 2x2x4 slice. The times are simulated.
32 devices in a mesh: rows: 8 (over z, y), wide: 4 (over x, core).
Axes of the slice: x: 2, y: 2, z: 4, core: 2. Of those that a mesh axis runs over, the one named last changes fastest.
Arguments:
- tokens: bfloat16 [16, 1024, 1024], P('rows', 'wide'), may hold values from -6 to 6
- doc_ids: int32 [16, 1024], P('rows'), may hold values from 0 to 5, never falling along the last dimension, each value on 1 to 512 neighbouring positions
- factor_weight: bfloat16 [1024, 800], replicated, may hold values from -0.3125 to 0.3125
- output_weight: bfloat16 [1024, 1024], replicated, may hold values from -0.5 to 0.5
- norm_one: float32 [1024], replicated, may hold values from 0.5 to 1.5
- norm_two: float32 [1024], replicated, may hold values from 0.5 to 1.5
- gate_weight: bfloat16 [1024, 2816], P(None, 'wide'), may hold values from -0.1875 to 0.1875
- up_weight: bfloat16 [1024, 2816], P(None, 'wide'), may hold values from -0.1875 to 0.1875
- down_weight: bfloat16 [2816, 1024], P('wide'), may hold values from -0.15625 to 0.15625
- cotangent: bfloat16 [16, 1024, 1024], P('rows', 'wide'), may hold values from -6 to 6
Outputs:
- output: bfloat16 [16, 1024, 1024], P('rows', 'wide')
- input_grad: bfloat16 [16, 1024, 1024], P('rows', 'wide')
- grad_factors: float32 [1024, 800], replicated
- grad_out: float32 [1024, 1024], replicated
- grad_norm_one: float32 [1024], replicated
- grad_norm_two: float32 [1024], replicated
- grad_gate: float32 [1024, 2816], P(None, 'wide')
- up_weight_gradient: float32 [1024, 2816], P(None, 'wide')
- down_weight_gradient: float32 [2816, 1024], P('wide')
Inputs may be any that keep to these rules, and one draw needn't show every extreme that they name: `doc_ids`: in each sequence the ids never fall along the positions; a document holds 1 to 512 positions, and one document of every sequence holds exactly 512.
All inputs are finite; a program needn't handle non-finite values.
Results may differ from a plain program's by a relative error of at most 0.017.
The roundings to bfloat16 on the way count: a program that leaves them out, or rounds other values in their place, can miss the bound.
Values may be sent and summed in bfloat16 or wider, within the bound.
A program may use at most 256 MiB of HBM per device.

v0:
```python
import jax
import jax.numpy as jnp
from jax import lax
from jax.sharding import PartitionSpec as P

H = 16
DH = 64
RQ = 6
RK = 2
SEQ_BLOCK = 2
EPS = 1e-06
NEG = -1000000000.0
MATMUL_EXACTNESS = lax.Precision.HIGHEST


def expand(part_a, part_b, heads, rank):
    leading = part_a.shape[:-1]
    left_part = part_a.reshape(leading + (heads, rank))
    right_part = part_b.reshape(leading + (rank, -1))
    return (
        jnp.einsum("...hr,...rd->...hd", left_part, right_part, preferred_element_type=jnp.float32)
        / rank
    )


def factor_grads(grad_heads, part_a, part_b, heads, rank):
    leading = part_a.shape[:-1]
    left_part = part_a.reshape(leading + (heads, rank)).astype(jnp.float32)
    right_part = part_b.reshape(leading + (rank, -1)).astype(jnp.float32)
    grad_left = (
        jnp.einsum("...hd,...rd->...hr", grad_heads, right_part, precision=MATMUL_EXACTNESS) / rank
    )
    grad_right = (
        jnp.einsum("...hd,...hr->...rd", grad_heads, left_part, precision=MATMUL_EXACTNESS) / rank
    )
    return (grad_left.reshape(leading + (-1,)), grad_right.reshape(leading + (-1,)))


def split_query(factor_rows):
    cut_one = H * RQ
    return (factor_rows[..., :cut_one], factor_rows[..., cut_one:])


def split_pair(factor_rows):
    cut_one = H * RK
    cut_two = cut_one + RK * DH
    cut_three = cut_two + H * RK
    return (
        factor_rows[..., :cut_one],
        factor_rows[..., cut_one:cut_two],
        factor_rows[..., cut_two:cut_three],
        factor_rows[..., cut_three:],
    )


def block_scores(queries, key_heads, allowed):
    scores = jnp.einsum(
        "sqhd,skhd->shqk", queries, key_heads, preferred_element_type=jnp.float32
    ) * DH ** (-0.5)
    return jnp.where(allowed[:, None], scores, NEG)


def attend_forward(block_parts):
    queries, key_heads, value_heads, allowed = block_parts
    scores = block_scores(queries, key_heads, allowed)
    row_top = jnp.max(scores, axis=-1, keepdims=True)
    exponent = jnp.exp(scores - row_top)
    totals = jnp.sum(exponent, axis=-1, keepdims=True)
    attn_probs = (exponent / totals).astype(jnp.bfloat16)
    mixed_out = jnp.einsum(
        "shqk,skhd->sqhd", attn_probs, value_heads, preferred_element_type=jnp.float32
    )
    return (mixed_out.astype(jnp.bfloat16), (row_top + jnp.log(totals))[..., 0])


def attend_backward(block_parts):
    queries, key_heads, value_heads, allowed, logsum, grad_mixed = block_parts
    scores = block_scores(queries, key_heads, allowed)
    attn_probs = jnp.exp(scores - logsum[..., None])
    grad_probs = jnp.einsum(
        "sqhd,skhd->shqk", grad_mixed, value_heads, preferred_element_type=jnp.float32
    )
    inner_sum = jnp.sum(attn_probs * grad_probs, axis=-1, keepdims=True)
    grad_scores = (attn_probs * (grad_probs - inner_sum)).astype(jnp.bfloat16)
    scaling = DH ** (-0.5)
    grad_query = (
        jnp.einsum("shqk,skhd->sqhd", grad_scores, key_heads, preferred_element_type=jnp.float32)
        * scaling
    )
    grad_key = (
        jnp.einsum("shqk,sqhd->skhd", grad_scores, queries, preferred_element_type=jnp.float32)
        * scaling
    )
    grad_value = jnp.einsum(
        "shqk,sqhd->skhd",
        attn_probs.astype(jnp.bfloat16),
        grad_mixed,
        preferred_element_type=jnp.float32,
    )
    return (grad_query, grad_key, grad_value)


def grouped(array_in):
    return array_in.reshape((array_in.shape[0] // SEQ_BLOCK, SEQ_BLOCK) + array_in.shape[1:])


def ungrouped(array_in):
    return array_in.reshape((array_in.shape[0] * array_in.shape[1],) + array_in.shape[2:])


def norm_backward(grad_normed, values, scaling, gain):
    weighted = grad_normed * gain
    grad_values = scaling * weighted - values * (scaling * scaling * scaling) * jnp.mean(
        weighted * values, axis=-1, keepdims=True
    )
    grad_gain = jnp.sum(grad_normed * values * scaling, axis=(0, 1))
    return (grad_values, grad_gain)


def body(
    tokens,
    doc_ids,
    factor_weight,
    output_weight,
    norm_one,
    norm_two,
    gate_weight,
    up_weight,
    down_weight,
    cotangent,
):
    seq_count, own_len, _unused = tokens.shape
    full_len = doc_ids.shape[1]
    offset = lax.axis_index("wide") * own_len
    query_columns = H * RQ + RQ * DH
    hidden_in = tokens.astype(jnp.float32)
    scale_one = lax.rsqrt(jnp.mean(hidden_in * hidden_in, axis=-1, keepdims=True) + EPS)
    first_normalized = (hidden_in * scale_one * norm_one).astype(jnp.bfloat16)
    normalized_total = lax.all_gather(first_normalized, "wide", axis=1, tiled=True)
    query_fac = jnp.einsum(
        "cnx,xo->cno",
        first_normalized,
        factor_weight[:, :query_columns],
        preferred_element_type=jnp.float32,
    ).astype(jnp.bfloat16)
    pair_fac = jnp.einsum(
        "cnx,xo->cno",
        normalized_total,
        factor_weight[:, query_columns:],
        preferred_element_type=jnp.float32,
    ).astype(jnp.bfloat16)
    query_a, query_b = split_query(query_fac)
    key_a, key_b, value_a, value_b = split_pair(pair_fac)
    queries = expand(query_a, query_b, H, RQ).astype(jnp.bfloat16)
    key_heads = expand(key_a, key_b, H, RK).astype(jnp.bfloat16)
    value_heads = expand(value_a, value_b, H, RK).astype(jnp.bfloat16)
    doc_query = lax.dynamic_slice_in_dim(doc_ids, offset, own_len, 1)
    key_pos = lax.broadcasted_iota(jnp.int32, (own_len, full_len), 1)
    query_pos = lax.broadcasted_iota(jnp.int32, (own_len, full_len), 0) + offset
    allowed = (doc_query[:, :, None] == doc_ids[:, None, :]) & (key_pos <= query_pos)[None]
    mixed_out, logsum = lax.map(
        attend_forward,
        (grouped(queries), grouped(key_heads), grouped(value_heads), grouped(allowed)),
    )
    attention_result = ungrouped(mixed_out).reshape(seq_count, own_len, H * DH)
    logsum = ungrouped(logsum)
    residual_branch = jnp.einsum(
        "trq,qx->trx", attention_result, output_weight, preferred_element_type=jnp.float32
    )
    hidden_middle = hidden_in + residual_branch
    scale_two = lax.rsqrt(jnp.mean(hidden_middle * hidden_middle, axis=-1, keepdims=True) + EPS)
    second_normalized = (hidden_middle * scale_two * norm_two).astype(jnp.bfloat16)
    input_rows_total = lax.all_gather(second_normalized, "wide", axis=1, tiled=True)
    gate_logits = jnp.einsum(
        "cnx,xo->cno", input_rows_total, gate_weight, preferred_element_type=jnp.float32
    )
    up_activation = jnp.einsum(
        "cnx,xo->cno", input_rows_total, up_weight, preferred_element_type=jnp.float32
    )
    gate_sig = jax.nn.sigmoid(gate_logits)
    feedforward_hidden = (gate_logits * gate_sig * up_activation).astype(jnp.bfloat16)
    partial_output = jnp.einsum(
        "gxk,km->gxm", feedforward_hidden, down_weight, preferred_element_type=jnp.float32
    )
    feed_out = lax.psum_scatter(
        partial_output.astype(jnp.bfloat16), "wide", scatter_dimension=1, tiled=True
    ).astype(jnp.float32)
    gradient_total = lax.all_gather(cotangent, "wide", axis=1, tiled=True)
    hidden_gradient = jnp.einsum(
        "uow,nw->uon", gradient_total, down_weight, preferred_element_type=jnp.float32
    )
    gate_logits_gradient = (
        hidden_gradient * up_activation * gate_sig * (1.0 + gate_logits * (1.0 - gate_sig))
    ).astype(jnp.bfloat16)
    up_logits_gradient = (hidden_gradient * gate_logits * gate_sig).astype(jnp.bfloat16)
    grad_in_part = jnp.einsum(
        "hnc,uc->hnu", gate_logits_gradient, gate_weight, preferred_element_type=jnp.float32
    )
    grad_in_part = grad_in_part + jnp.einsum(
        "hnc,uc->hnu", up_logits_gradient, up_weight, preferred_element_type=jnp.float32
    )
    grad_normed_two = lax.psum_scatter(
        grad_in_part.astype(jnp.bfloat16), "wide", scatter_dimension=1, tiled=True
    ).astype(jnp.float32)
    grad_gate = jnp.einsum(
        "wvm,wvu->mu", input_rows_total, gate_logits_gradient, preferred_element_type=jnp.float32
    )
    up_weight_gradient = jnp.einsum(
        "wvm,wvu->mu", input_rows_total, up_logits_gradient, preferred_element_type=jnp.float32
    )
    down_weight_gradient = jnp.einsum(
        "qmw,qmv->wv", feedforward_hidden, gradient_total, preferred_element_type=jnp.float32
    )
    grad_gate, up_weight_gradient, down_weight_gradient = (
        lax.psum(grad_gate.astype(jnp.bfloat16), "rows").astype(jnp.float32),
        lax.psum(up_weight_gradient.astype(jnp.bfloat16), "rows").astype(jnp.float32),
        lax.psum(down_weight_gradient.astype(jnp.bfloat16), "rows").astype(jnp.float32),
    )
    output = (hidden_middle + feed_out).astype(jnp.bfloat16)
    grad_mid_norm, gain_two = norm_backward(grad_normed_two, hidden_middle, scale_two, norm_two)
    grad_mid = cotangent.astype(jnp.float32) + grad_mid_norm
    branch_gradient = grad_mid.astype(jnp.bfloat16)
    grad_w_out = jnp.einsum(
        "amx,amb->xb", attention_result, branch_gradient, preferred_element_type=jnp.float32
    )
    grad_attended = jnp.einsum(
        "pjk,zk->pjz", branch_gradient, output_weight, preferred_element_type=jnp.float32
    ).astype(jnp.bfloat16)
    grad_attended = grad_attended.reshape(seq_count, own_len, H, DH)
    grad_query, grad_key, grad_value = lax.map(
        attend_backward,
        (
            grouped(queries),
            grouped(key_heads),
            grouped(value_heads),
            grouped(allowed),
            grouped(logsum),
            grouped(grad_attended),
        ),
    )
    grad_query = ungrouped(grad_query)
    grad_key = ungrouped(grad_key)
    grad_value = ungrouped(grad_value)
    grad_qa, grad_qb = factor_grads(grad_query, query_a, query_b, H, RQ)
    grad_ka, grad_kb = factor_grads(grad_key, key_a, key_b, H, RK)
    grad_va, grad_vb = factor_grads(grad_value, value_a, value_b, H, RK)
    pair_grads = jnp.concatenate([grad_ka, grad_kb, grad_va, grad_vb], axis=-1)
    pair_own = lax.psum_scatter(
        pair_grads.astype(jnp.bfloat16), "wide", scatter_dimension=1, tiled=True
    ).astype(jnp.float32)
    factor_gradient = jnp.concatenate([grad_qa, grad_qb, pair_own], axis=-1).astype(jnp.bfloat16)
    grad_w_factors = jnp.einsum(
        "wvm,wvu->mu", first_normalized, factor_gradient, preferred_element_type=jnp.float32
    )
    grad_normed_one = jnp.einsum(
        "hnc,uc->hnu", factor_gradient, factor_weight, preferred_element_type=jnp.float32
    )
    grad_in_norm, gain_one = norm_backward(grad_normed_one, hidden_in, scale_one, norm_one)
    input_grad = (grad_mid + grad_in_norm).astype(jnp.bfloat16)
    grad_w_factors, grad_w_out, gain_one, gain_two = lax.psum(
        (grad_w_factors, grad_w_out, gain_one, gain_two), ("rows", "wide")
    )
    return (
        output,
        input_grad,
        grad_w_factors,
        grad_w_out,
        gain_one,
        gain_two,
        grad_gate,
        up_weight_gradient,
        down_weight_gradient,
    )


def solution(mesh):
    placed = (
        P("rows", "wide", None),
        P("rows", None),
        P(),
        P(),
        P(),
        P(),
        P(None, "wide"),
        P(None, "wide"),
        P("wide", None),
        P("rows", "wide", None),
    )
    return jax.shard_map(
        body,
        mesh=mesh,
        in_specs=placed,
        out_specs=(
            P("rows", "wide", None),
            P("rows", "wide", None),
            P(),
            P(),
            P(),
            P(),
            P(None, "wide"),
            P(None, "wide"),
            P("wide", None),
        ),
        check_vma=False,
    )
```

profile of v0, /device:TPU:0, one launch (start us, length us, event | category | flops | bytes accessed | tf_op | source)
XLA Modules:
  0.0 899.3 jit_solution(4847978893055860476)
XLA Ops:
  22.8 5.3 copy.91
  29.6 20.3 %all-gather.4.cloned.1.call-done = bf16[2,1024,1024]{2,1,0:T(8,128)(2,1)} async-done(((bf16[2,256,1024]{2,1,0:T(8,128)(2,1)}), bf16[2,1024,1024]{2,1,0:T(8,128)(2,1)}) %all-gather.4.cloned.1.call-update) | async-done | bytes 4194320 | tf_op jit(solution)/shard_map/all_gather | solution.py:139
  59.4 7.8 fusion.68
  67.3 12.8 %copy.94 = f32[2,1024,16,64]{1,3,2,0:T(8,128)} copy(f32[2,1024,16,64]{3,2,1,0:T(8,128)} %fusion.68) | data formatting | bytes 16777216 | tf_op jit(solution)/shard_map/...hr,...rd->...hd/dot_general | solution.py:21
  84.6 7.8 fusion.66
  92.5 12.8 %copy.87 = f32[2,1024,16,64]{1,3,2,0:T(8,128)} copy(f32[2,1024,16,64]{3,2,1,0:T(8,128)} %fusion.66) | data formatting | bytes 16777216 | tf_op jit(solution)/shard_map/...hr,...rd->...hd/dot_general | solution.py:21
  105.3 17.1 %fusion.65 = (f32[2,16,256]{2,1,0:T(8,128)S(1)}, f32[2,16,256,1024]{3,2,1,0:T(8,128)}) fusion(f32[2,1024,16,64]{1,3,2,0:T(8,128)} %copy.94, f32[2,256,16,64]{1,3,2,0:T(8,128)} %copy.91, pred[2,256,1024]{2,1,0:T(8,128)(4,1)} %compare_and_fusion), kind=kOutput, calls=%fused_computation.112 | convolution fusion | flops 1104142336 | bytes 44597248 | tf_op jit(solution)/shard_map/while/body/eval_jaxpr/sqhd,skhd->shqk/dot_general | solution.py:57
  122.4 14.7 %fusion = f32[2,16,256]{2,1,0:T(8,128)S(1)} fusion(f32[2,16,256,1024]{3,2,1,0:T(8,128)} %get-tuple-element.85, f32[2,16,256]{2,1,0:T(8,128)S(1)} %get-tuple-element.84), kind=kLoop, calls=%fused_computation.6 | loop fusion | flops 16769024 | bytes 33619968 | tf_op jit(solution)/shard_map/while/body/eval_jaxpr/reduce_sum | solution.py:68
  137.1 13.2 %fusion.38 = bf16[2,16,64,256]{3,2,1,0:T(8,128)(2,1)S(1)} fusion(f32[2,16,256,1024]{3,2,1,0:T(8,128)} %get-tuple-element.85, f32[2,16,256]{2,1,0:T(8,128)S(1)} %fusion, f32[2,16,256]{2,1,0:T(8,128)S(1)} %get-tuple-element.84, f32[2,1024,16,64]{1,3,2,0:T(8,128)S(1)} %copy-done.4), kind=kOutput, calls=%fused_computation.67 | convolution fusion | flops 1103626240 | bytes 43057152 | tf_op jit(solution)/shard_map/while/body/eval_jaxpr/shqk,skhd->sqhd/dot_general | solution.py:70
  155.1 33.8 %all-gather.6.cloned.1.call-done = bf16[2,1024,1024]{2,1,0:T(8,128)(2,1)} async-done(((bf16[2,256,1024]{2,1,0:T(8,128)(2,1)}), bf16[2,1024,1024]{2,1,0:T(8,128)(2,1)}) %all-gather.6.cloned.1.call-update) | async-done | bytes 4194320 | tf_op jit(solution)/shard_map/all_gather | solution.py:173
  188.9 8.4 fusion.43
  202.4 22.6 %all-gather.8.cloned.1.call-done = bf16[2,1024,1024]{2,1,0:T(8,128)(2,1)} async-done(((bf16[2,256,1024]{2,1,0:T(8,128)(2,1)}), bf16[2,1024,1024]{2,1,0:T(8,128)(2,1)}) %all-gather.8.cloned.1.call-update) | async-done | bytes 4194320 | tf_op jit(solution)/shard_map/all_gather | solution.py:188
  225.0 10.3 %multiply_convert_fusion.3 = (bf16[2,1024,704]{1,2,0:T(8,128)(2,1)S(1)}, bf16[2,1024,704]{1,2,0:T(8,128)(2,1)S(1)}, bf16[2,1024,704]{1,2,0:T(8,128)(2,1)}) fusion(f32[2,1024,704]{1,2,0:T(8,128)} %fusion.47, f32[2,1024,704]{1,2,0:T(8,128)} %fusion.43, bf16[2,1024,1024]{2,1,0:T(8,128)(2,1)} %all-gather.8.cloned.1.call-done, bf16[704,1024]{1,0:T(8,128)(2,1)} %param.18), kind=kOutput, calls=%fused_computation.15 | convolution fusion | flops 2975858688 | bytes 25821184 | tf_op jit(solution)/shard_map/uow,nw->uon/dot_general | solution.py:189
  244.2 7.8 convolution_convert_fusion
  252.1 36.6 %reduce-scatter.6.cloned.1.call-done = bf16[2,256,1024]{2,1,0:T(8,128)(2,1)} async-done(((bf16[2,1024,1024]{2,1,0:T(8,128)(2,1)}), bf16[2,256,1024]{2,1,0:T(8,128)(2,1)}) %reduce-scatter.6.cloned.1.call-update) | async-done | bytes 1048592 | tf_op jit(solution)/shard_map/reduce_scatter | solution.py:202
  291.9 43.8 %reduce-scatter.4.cloned.1.call-done = bf16[2,256,1024]{2,1,0:T(8,128)(2,1)} async-done(((bf16[2,1024,1024]{2,1,0:T(8,128)(2,1)}), bf16[2,256,1024]{2,1,0:T(8,128)(2,1)}) %reduce-scatter.4.cloned.1.call-update) | async-done | bytes 1048592 | tf_op jit(solution)/shard_map/reduce_scatter | solution.py:185
  343.1 25.8 %multiply_reduce_fusion = (f32[2,16,256]{2,1,0:T(8,128)S(1)}, f32[2,16,256,1024]{3,2,1,0:T(8,128)}) fusion(f32[2,16,256,1024]{3,2,1,0:T(8,128)} %get-tuple-element.85, f32[2,16,256]{2,1,0:T(8,128)S(1)} %log_add_fusion, bf16[2,256,16,64]{1,3,2,0:T(8,128)(2,1)S(1)} %bitcast.112, f32[2,1024,16,64]{1,3,2,0:T(8,128)} %copy.87), kind=kOutput, calls=%fused_computation.1 | convolution fusion | flops 1103093760 | bytes 76611584 | tf_op jit(solution)/shard_map/while/body/eval_jaxpr/sqhd,skhd->shqk/dot_general | solution.py:80
  368.9 27.9 %multiply_convert_fusion = bf16[2,16,256,1024]{3,2,1,0:T(8,128)(2,1)} fusion(f32[2,16,256,1024]{3,2,1,0:T(8,128)} %get-tuple-element.89, f32[2,16,256,1024]{3,2,1,0:T(8,128)} %get-tuple-element.85, f32[2,16,256]{2,1,0:T(8,128)S(1)} %get-tuple-element.88, f32[2,16,256]{2,1,0:T(8,128)S(1)} %log_add_fusion), kind=kLoop, calls=%fused_computation | loop fusion | flops 33554432 | bytes 83951616 | tf_op jit(solution)/shard_map/while/body/eval_jaxpr/convert_element_type | solution.py:84
  396.8 12.0 %multiply_bitcast_fusion = f32[2,1024,16,64]{1,3,2,0:T(8,128)} fusion(bf16[2,16,256,1024]{3,2,1,0:T(8,128)(2,1)} %multiply_convert_fusion, f32[2,256,16,64]{1,3,2,0:T(8,128)S(1)} %copy-done.6), kind=kOutput, calls=%fused_computation.11 | convolution fusion | flops 1076887552 | bytes 27262976 | tf_op jit(solution)/shard_map/while/body/eval_jaxpr/shqk,sqhd->skhd/dot_general | solution.py:91
  408.9 14.6 %copy.104 = f32[2,1024,16,64]{3,2,1,0:T(8,128)} copy(f32[2,1024,16,64]{1,3,2,0:T(8,128)} %multiply_bitcast_fusion) | data formatting | bytes 16777216 | tf_op jit(solution)/shard_map/while/body/eval_jaxpr/mul | solution.py:91
  423.5 17.1 %fusion.70 = f32[2,1024,16,2]{2,3,1,0:T(2,128)} fusion(f32[2,1024,16,64]{3,2,1,0:T(8,128)} %copy.104, bf16[2,1024,2,64]{3,2,1,0:T(2,128)(2,1)S(1)} %copy-done.14), kind=kOutput, calls=%fused_computation.117 | convolution fusion | flops 50331648 | bytes 9175040 | tf_op jit(solution)/shard_map/...hd,...rd->...hr/dot_general | solution.py:31
  440.7 9.6 %fusion.71 = f32[2,1024,2,64]{3,2,1,0:T(2,128)} fusion(bf16[2,1024,16,2]{2,3,1,0:T(2,128)(2,1)S(1)} %copy-done.15, f32[2,1024,16,64]{3,2,1,0:T(8,128)S(1)} %copy-done.2), kind=kOutput, calls=%fused_computation.118 | convolution fusion | flops 50331648 | bytes 9568256 | tf_op jit(solution)/shard_map/...hd,...hr->...rd/dot_general | solution.py:34
  450.3 16.8 %fusion.6 = f32[2,1024,16,64]{1,3,2,0:T(8,128)} fusion(bf16[2,256,16,64]{1,3,2,0:T(8,128)(2,1)S(1)} %bitcast.113, f32[2,16,256,1024]{3,2,1,0:T(8,128)} %get-tuple-element.85, f32[2,16,256]{2,1,0:T(8,128)S(1)} %log_add_fusion), kind=kOutput, calls=%fused_computation.25 | convolution fusion | flops 1090519040 | bytes 43024384 | tf_op jit(solution)/shard_map/while/body/eval_jaxpr/shqk,sqhd->skhd/dot_general | solution.py:94
  467.1 14.6 %copy.111 = f32[2,1024,16,64]{3,2,1,0:T(8,128)} copy(f32[2,1024,16,64]{1,3,2,0:T(8,128)} %fusion.6) | data formatting | bytes 16777216 | tf_op jit(solution)/shard_map/while/body/eval_jaxpr/shqk,sqhd->skhd/transpose | solution.py:94
  481.7 17.1 %fusion.72 = f32[2,1024,16,2]{2,3,1,0:T(2,128)} fusion(f32[2,1024,16,64]{3,2,1,0:T(8,128)} %copy.111, bf16[2,1024,2,64]{3,2,1,0:T(2,128)(2,1)S(1)} %copy-done.12), kind=kOutput, calls=%fused_computation.119 | convolution fusion | flops 50331648 | bytes 9175040 | tf_op jit(solution)/shard_map/...hd,...rd->...hr/dot_general | solution.py:31
  498.8 9.8 %fusion.73 = f32[2,1024,2,64]{3,2,1,0:T(2,128)} fusion(bf16[2,1024,16,2]{2,3,1,0:T(2,128)(2,1)S(1)} %copy-done.16, f32[2,1024,16,64]{3,2,1,0:T(8,128)S(1)} %copy-done.3), kind=kOutput, calls=%fused_computation.120 | convolution fusion | flops 50331648 | bytes 9568256 | tf_op jit(solution)/shard_map/...hd,...hr->...rd/dot_general | solution.py:34
  519.6 7.6 bitcast_convert_fusion.1
  535.7 12.4 %multiply_bitcast_fusion.1 = f32[2,256,16,64]{1,3,2,0:T(8,128)} fusion(bf16[2,16,256,1024]{3,2,1,0:T(8,128)(2,1)} %multiply_convert_fusion, f32[2,1024,16,64]{1,3,2,0:T(8,128)} %copy.94), kind=kOutput, calls=%fused_computation.55 | convolution fusion | flops 1078460416 | bytes 27262976 | tf_op jit(solution)/shard_map/while/body/eval_jaxpr/shqk,skhd->sqhd/dot_general | solution.py:87
  553.3 6.9 fusion.69
  576.8 133.3 %all-reduce.8.cloned.1.call-done = (bf16[1024,704]{0,1:T(8,128)(2,1)}, bf16[1024,704]{0,1:T(8,128)(2,1)}, bf16[704,1024]{1,0:T(8,128)(2,1)}) async-done(((bf16[1024,704]{0,1:T(8,128)(2,1)}, bf16[1024,704]{0,1:T(8,128)(2,1)}, bf16[704,1024]{1,0:T(8,128)(2,1)}), (bf16[1024,704]{0,1:T(8,128)(2,1)}, bf16[1024,704]{0,1:T(8,128)(2,1)}, bf16[704,1024]{1,0:T(8,128)(2,1)})) %all-reduce.8.cloned.1.call-update) | async-done | bytes 4325392 | tf_op jit(solution)/shard_map/psum | solution.py:215
  721.2 40.9 %all-reduce = (f32[1024]{0:T(1024)}, f32[1024]{0:T(1024)}) all-reduce(f32[1024]{0:T(1024)S(1)} %get-tuple-element.52, f32[1024]{0:T(1024)S(1)} %copy-done.34), channel_id=1, replica_groups=mesh['rows'=8,'wide'=4] {'rows','wide'}, use_global_device_ids=true, to_apply=%region_13.14 | all-reduce | flops 2048 | bytes 16384 | tf_op jit(solution)/shard_map/psum | solution.py:260
  765.9 120.0 %all-reduce.6.cloned.1.call-done = (f32[1024,800]{0,1:T(8,128)}, f32[1024,1024]{1,0:T(8,128)}) async-done(((f32[1024,800]{0,1:T(8,128)}, f32[1024,1024]{1,0:T(8,128)}), (f32[1024,800]{0,1:T(8,128)}, f32[1024,1024]{1,0:T(8,128)})) %all-reduce.6.cloned.1.call-update) | async-done | bytes 7471120 | tf_op jit(solution)/shard_map/psum | solution.py:260
  (184 shorter events, 122.5 us)
Async XLA Ops:
  7.2 143.2 %copy-start = (bf16[1024,1024]{1,0:T(8,128)(2,1)S(1)}, bf16[1024,1024]{1,0:T(8,128)(2,1)}, u32[]{:S(2)}) copy-start(bf16[1024,1024]{1,0:T(8,128)(2,1)} %param.13) | copy-start | bytes 6291460
  7.2 42.7 %all-gather.4.cloned.1.call-start = ((), (), s32[]{:S(2)}) async-start(), calls=%async_computation.3 | async-start | bytes 5242880 | tf_op jit(solution)/shard_map/all_gather | solution.py:139
  12.6 176.3 %all-gather.6.cloned.1.call-start = ((), (), s32[]{:S(2)}) async-start(), calls=%async_computation.4 | async-start | bytes 5242880 | tf_op jit(solution)/shard_map/all_gather | solution.py:173
  16.1 6.7 copy-start.17
  22.8 5.3 copy-start.36
  57.3 10.0 %copy-start.13 = (bf16[2,1024,2,64]{3,2,1,0:T(2,128)(2,1)}, bf16[2,1024,2,64]{3,2,1,0:T(2,128)(2,1)S(1)}, u32[]{:S(2)}) copy-start(bf16[2,1024,2,64]{3,2,1,0:T(2,128)(2,1)S(1)} %copy.93) | copy-start | bytes 1572868
  82.4 10.0 %copy-start.11 = (bf16[2,1024,2,64]{3,2,1,0:T(2,128)(2,1)}, bf16[2,1024,2,64]{3,2,1,0:T(2,128)(2,1)S(1)}, u32[]{:S(2)}) copy-start(bf16[2,1024,2,64]{3,2,1,0:T(2,128)(2,1)S(1)} %copy.86) | copy-start | bytes 1572868
  122.4 14.7 %copy-start.4 = (f32[2,1024,16,64]{1,3,2,0:T(8,128)S(1)}, f32[2,1024,16,64]{1,3,2,0:T(8,128)}, u32[]{:S(2)}) copy-start(f32[2,1024,16,64]{1,3,2,0:T(8,128)} %copy.87) | copy-start | bytes 25165828
  137.1 13.2 %copy-start.7 = (bf16[2,256,1024]{2,1,0:T(8,128)(2,1)S(1)}, bf16[2,256,1024]{2,1,0:T(8,128)(2,1)}, u32[]{:S(2)}) copy-start(bf16[2,256,1024]{2,1,0:T(8,128)(2,1)} %param.10) | copy-start | bytes 3145732
  154.3 70.7 %all-gather.8.cloned.1.call-start = ((), (), s32[]{:S(2)}) async-start(), calls=%async_computation.6 | async-start | bytes 5242880 | tf_op jit(solution)/shard_map/all_gather | solution.py:188
  155.0 133.7 %reduce-scatter.6.cloned.1.call-start = ((), (), s32[]{:S(2)}) async-start(), calls=%async_computation.7 | async-start | bytes 5242880 | tf_op jit(solution)/shard_map/reduce_scatter | solution.py:202
  188.9 8.4 copy-start.38
  188.9 8.4 copy-start.42
  225.0 10.4 %copy-start.43 = (bf16[1024,704]{0,1:T(8,128)(2,1)S(1)}, bf16[1024,704]{0,1:T(8,128)(2,1)}, u32[]{:S(2)}) copy-start(bf16[1024,704]{0,1:T(8,128)(2,1)} %param.16) | copy-start | bytes 4325380
  244.0 91.7 %reduce-scatter.4.cloned.1.call-start = ((), (), s32[]{:S(2)}) async-start(), calls=%async_computation.5 | async-start | bytes 5242880 | tf_op jit(solution)/shard_map/reduce_scatter | solution.py:185
  252.0 83.7 %copy-start.25 = (bf16[2,256,1024]{2,1,0:T(8,128)(2,1)S(1)}, bf16[2,256,1024]{2,1,0:T(8,128)(2,1)}, u32[]{:S(2)}) copy-start(bf16[2,256,1024]{2,1,0:T(8,128)(2,1)} %param.19) | copy-start | bytes 3145732
  252.0 321.1 %reduce-scatter.8.cloned.1.call-start = ((), (), s32[]{:S(2)}) async-start(), calls=%async_computation.8 | async-start | bytes 1638400 | tf_op jit(solution)/shard_map/reduce_scatter | solution.py:248
  343.1 25.8 %copy-start.9 = (bf16[2,256,1024]{1,2,0:T(8,128)(2,1)}, bf16[2,256,1024]{1,2,0:T(8,128)(2,1)S(1)}, u32[]{:S(2)}) copy-start(bf16[2,256,1024]{1,2,0:T(8,128)(2,1)S(1)} %copy.96) | copy-start | bytes 3145732
  368.9 27.9 %copy-start.6 = (f32[2,256,16,64]{1,3,2,0:T(8,128)S(1)}, f32[2,256,16,64]{1,3,2,0:T(8,128)}, u32[]{:S(2)}) copy-start(f32[2,256,16,64]{1,3,2,0:T(8,128)} %copy.91) | copy-start | bytes 6291460
  408.8 14.7 %copy-start.14 = (bf16[2,1024,2,64]{3,2,1,0:T(2,128)(2,1)S(1)}, bf16[2,1024,2,64]{3,2,1,0:T(2,128)(2,1)}, u32[]{:S(2)}) copy-start(bf16[2,1024,2,64]{3,2,1,0:T(2,128)(2,1)} %copy-done.13) | copy-start | bytes 1572868
  423.5 17.2 %copy-start.2 = (f32[2,1024,16,64]{3,2,1,0:T(8,128)S(1)}, f32[2,1024,16,64]{3,2,1,0:T(8,128)}, u32[]{:S(2)}) copy-start(f32[2,1024,16,64]{3,2,1,0:T(8,128)} %copy.104) | copy-start | bytes 25165828
  423.5 17.2 %copy-start.15 = (bf16[2,1024,16,2]{2,3,1,0:T(2,128)(2,1)S(1)}, bf16[2,1024,16,2]{2,3,1,0:T(2,128)(2,1)}, u32[]{:S(2)}) copy-start(bf16[2,1024,16,2]{2,3,1,0:T(2,128)(2,1)} %copy.92) | copy-start | bytes 393220
  440.7 9.6 %copy-start.10 = (bf16[2,256,1024]{1,2,0:T(8,128)(2,1)S(1)}, bf16[2,256,1024]{1,2,0:T(8,128)(2,1)}, u32[]{:S(2)}) copy-start(bf16[2,256,1024]{1,2,0:T(8,128)(2,1)} %copy-done.9) | copy-start | bytes 3145732
  467.1 14.6 %copy-start.12 = (bf16[2,1024,2,64]{3,2,1,0:T(2,128)(2,1)S(1)}, bf16[2,1024,2,64]{3,2,1,0:T(2,128)(2,1)}, u32[]{:S(2)}) copy-start(bf16[2,1024,2,64]{3,2,1,0:T(2,128)(2,1)} %copy-done.11) | copy-start | bytes 1572868
  481.7 17.1 %copy-start.3 = (f32[2,1024,16,64]{3,2,1,0:T(8,128)S(1)}, f32[2,1024,16,64]{3,2,1,0:T(8,128)}, u32[]{:S(2)}) copy-start(f32[2,1024,16,64]{3,2,1,0:T(8,128)} %copy.111) | copy-start | bytes 25165828
  481.7 17.1 %copy-start.16 = (bf16[2,1024,16,2]{2,3,1,0:T(2,128)(2,1)S(1)}, bf16[2,1024,16,2]{2,3,1,0:T(2,128)(2,1)}, u32[]{:S(2)}) copy-start(bf16[2,1024,16,2]{2,3,1,0:T(2,128)(2,1)} %copy.85) | copy-start | bytes 393220
  519.6 190.5 %all-reduce.8.cloned.1.call-start = ((), (), s32[]{:S(2)}) async-start(), calls=%async_computation.10 | async-start | bytes 8650752 | tf_op jit(solution)/shard_map/psum | solution.py:215
  519.6 7.6 copy-start.39
  519.6 7.6 copy-start.49
  535.7 350.3 %all-reduce.6.cloned.1.call-start = ((), (), s32[]{:S(2)}) async-start(), calls=%async_computation.9 | async-start | bytes 14942208 | tf_op jit(solution)/shard_map/psum | solution.py:260
  718.3 43.8 %copy-start.37 = (f32[2,256]{1,0:T(2,128)S(1)}, f32[2,256]{1,0:T(2,128)}, u32[]{:S(2)}) copy-start(f32[2,256]{1,0:T(2,128)} %get-tuple-element.80) | copy-start | bytes 6148
  886.0 6.2 copy-start.1
  (26 other events, 80.3 us)
Sparse Core Ops, SparseCore 0:
  12.7 37.1 all-gather.3
  154.4 34.4 all-gather.5
  190.5 34.4 all-gather.7
  244.1 44.5 reduce-scatter.5
  291.1 44.5 reduce-scatter.3
  519.7 26.4 reduce-scatter.7
  550.6 159.4 all-reduce.7
  716.7 169.1 all-reduce.5
where the time goes:
time: 904 us; the launch traced here: 899 us
  waiting for transfers between devices  411 us (45%)
  matrix products  259 us (29%)
  local copies, waits for them, and re-layouts  102 us (11%)
  other arithmetic  71.4 us (8%)
  blocking collectives  40.9 us (5%)
  between operations  14.9 us (2%)
    psum x1, waiting for transfers between devices, body(): lax.psum(grad_gate.astype(jnp.bfloat16), 'rows').astype(jnp.float32)  133 us
    psum x1, waiting for transfers between devices, body(): lax.psum((grad_w_factors, grad_w_out, gain_one, gain_two), ('rows', 'wide'))  120 us
    reduce_scatter x1, waiting for transfers between devices, body(): lax.psum_scatter(partial_output.astype(jnp.bfloat16), 'wide', scatter_dim...  43.8 us
    dot_general x3, matrix products, factor_grads(): jnp.einsum('...hd,...rd->...hr', grad_heads, right_part, precision=MATMUL...  41.1 us
    psum x1, blocking collectives, body(): lax.psum((grad_w_factors, grad_w_out, gain_one, gain_two), ('rows', 'wide'))  40.9 us
    reduce_scatter x1, waiting for transfers between devices, body(): lax.psum_scatter(grad_in_part.astype(jnp.bfloat16), 'wide', scatter_dimen...  36.6 us
    all_gather x1, waiting for transfers between devices, body(): lax.all_gather(second_normalized, 'wide', axis=1, tiled=True)  33.8 us
    dot_general x3, local copies, waits for them, and re-layouts, expand(): jnp.einsum('...hr,...rd->...hd', left_part, right_part, preferred_element...  31 us
  transfers between devices with their start and end apart: 8, of which 7 were waited for; matrix products, arithmetic and copies ran while one was open for 12% of the time, Pallas kernels for 0%

commit v1 on v0

--- a/solution.py
+++ b/solution.py
@@ -11,6 +11,31 @@
 EPS = 1e-06
 NEG = -1000000000.0
 MATMUL_EXACTNESS = lax.Precision.HIGHEST
+
+
+def units_list(slab_in, array_axis):
+    slab_in = jnp.moveaxis(slab_in, 0, array_axis)
+    after = slab_in.shape
+    seen_now = slab_in.reshape(
+        *after[:array_axis], after[array_axis] * after[array_axis + 1], *after[array_axis + 2 :]
+    )
+    return seen_now
+
+
+def hold_the_sites(xx, axis_id, dim_i=1):
+    how_many = lax.axis_size(axis_id)
+    mat_out = range(how_many)
+    carry_out = map(lambda q: (q, (q + 1) % how_many), mat_out)
+    row_list = list(carry_out)
+    trail = [xx]
+    while len(trail) < how_many:
+        state_next = lax.ppermute(trail[-1], axis_name=axis_id, perm=row_list)
+        trail.append(state_next)
+    y1 = lax.axis_index(axis_id)
+    everything = jnp.stack(trail)
+    trail = everything[(y1 - jnp.arange(how_many)) % how_many]
+    x_new = units_list(trail, dim_i)
+    return x_new
 
 
 def expand(part_a, part_b, heads, rank):
@@ -136,7 +161,7 @@
     hidden_in = tokens.astype(jnp.float32)
     scale_one = lax.rsqrt(jnp.mean(hidden_in * hidden_in, axis=-1, keepdims=True) + EPS)
     first_normalized = (hidden_in * scale_one * norm_one).astype(jnp.bfloat16)
-    normalized_total = lax.all_gather(first_normalized, "wide", axis=1, tiled=True)
+    normalized_total = hold_the_sites(first_normalized, "wide")
     query_fac = jnp.einsum(
         "cnx,xo->cno",
         first_normalized,

time: 904 us -> 924 us (1.022)
    ppermute x0 -> x3, waiting for transfers between devices: none -> 27.1 us  [hold_the_sites(): state_next = lax.ppermute(trail[-1], axis_name=axis_id, perm=row_list)]
    all_gather x1 -> x0, waiting for transfers between devices: 20.3 us -> none  [body(): lax.all_gather(first_normalized, 'wide', axis=1, tiled=True)]
  transfers between devices with their start and end apart: 8 -> 10, of which waited for: 7 -> 9; matrix products, arithmetic and copies ran while one was open for 12% -> 12% of each run, Pallas kernels for 0% -> 0%
where the time goes in v1:
time: 924 us; the launch traced here: 919 us
  waiting for transfers between devices  420 us (45%)
  matrix products  256 us (28%)
  local copies, waits for them, and re-layouts  110 us (12%)
  other arithmetic  74.3 us (8%)
  blocking collectives  40.9 us (4%)
  between operations  14.9 us (2%)
    psum x1, waiting for transfers between devices, body(): lax.psum(grad_gate.astype(jnp.bfloat16), 'rows').astype(jnp.float32)  133 us
    psum x1, waiting for transfers between devices, body(): lax.psum((grad_w_factors, grad_w_out, gain_one, gain_two), ('rows', 'wide'))  120 us
    reduce_scatter x1, waiting for transfers between devices, body(): lax.psum_scatter(partial_output.astype(jnp.bfloat16), 'wide', scatter_dim...  43.8 us
    dot_general x3, matrix products, factor_grads(): jnp.einsum('...hd,...rd->...hr', grad_heads, right_part, precision=MATMUL...  41.1 us
    psum x1, blocking collectives, body(): lax.psum((grad_w_factors, grad_w_out, gain_one, gain_two), ('rows', 'wide'))  40.9 us
    reduce_scatter x1, waiting for transfers between devices, body(): lax.psum_scatter(grad_in_part.astype(jnp.bfloat16), 'wide', scatter_dimen...  36.4 us
    all_gather x1, waiting for transfers between devices, body(): lax.all_gather(second_normalized, 'wide', axis=1, tiled=True)  35.9 us
    dot_general x3, local copies, waits for them, and re-layouts, expand(): jnp.einsum('...hr,...rd->...hd', left_part, right_part, preferred_element...  30.2 us
  transfers between devices with their start and end apart: 10, of which 9 were waited for; matrix products, arithmetic and copies ran while one was open for 12% of the time, Pallas kernels for 0%

profile of v1, /device:TPU:0, one launch (start us, length us, event | category | flops | bytes accessed | tf_op | source)
XLA Modules:
  0.0 918.5 jit_solution(8641462877340204601)
XLA Ops:
  11.6 14.5 %collective-permute-done = bf16[2,256,1024]{2,1,0:T(8,128)(2,1)} collective-permute-done((bf16[2,256,1024]{2,1,0:T(8,128)(2,1)S(1)}, bf16[2,256,1024]{2,1,0:T(8,128)(2,1)}, u32[]{:S(2)}, u32[]{:S(2)}) %collective-permute-start) | collective-permute-done | bytes 1048608 | tf_op jit(solution)/shard_map/ppermute | solution.py:32
  43.9 11.3 %collective-permute-done.2 = bf16[2,256,1024]{2,1,0:T(8,128)(2,1)S(1)} collective-permute-done((bf16[2,256,1024]{2,1,0:T(8,128)(2,1)}, bf16[2,256,1024]{2,1,0:T(8,128)(2,1)S(1)}, u32[]{:S(2)}, u32[]{:S(2)}) %collective-permute-start.2) | collective-permute-done | bytes 1048608 | tf_op jit(solution)/shard_map/ppermute | solution.py:32
  75.7 8.0 fusion.70
  83.6 12.8 %copy.96 = f32[2,1024,16,64]{1,3,2,0:T(8,128)} copy(f32[2,1024,16,64]{3,2,1,0:T(8,128)} %fusion.70) | data formatting | bytes 16777216 | tf_op jit(solution)/shard_map/...hr,...rd->...hd/dot_general | solution.py:46
  102.0 8.0 fusion.68
  110.0 12.8 %copy.89 = f32[2,1024,16,64]{1,3,2,0:T(8,128)} copy(f32[2,1024,16,64]{3,2,1,0:T(8,128)} %fusion.68) | data formatting | bytes 16777216 | tf_op jit(solution)/shard_map/...hr,...rd->...hd/dot_general | solution.py:46
  122.8 17.1 %fusion.67 = (f32[2,16,256]{2,1,0:T(8,128)S(1)}, f32[2,16,256,1024]{3,2,1,0:T(8,128)}) fusion(f32[2,1024,16,64]{1,3,2,0:T(8,128)} %copy.96, f32[2,256,16,64]{1,3,2,0:T(8,128)} %copy.93, pred[2,256,1024]{2,1,0:T(8,128)(4,1)} %compare_and_fusion), kind=kOutput, calls=%fused_computation.121 | convolution fusion | flops 1104142336 | bytes 44597248 | tf_op jit(solution)/shard_map/while/body/eval_jaxpr/sqhd,skhd->shqk/dot_general | solution.py:82
  139.9 14.7 %fusion = f32[2,16,256]{2,1,0:T(8,128)S(1)} fusion(f32[2,16,256,1024]{3,2,1,0:T(8,128)} %get-tuple-element.85, f32[2,16,256]{2,1,0:T(8,128)S(1)} %get-tuple-element.84), kind=kLoop, calls=%fused_computation.7 | loop fusion | flops 16769024 | bytes 33619968 | tf_op jit(solution)/shard_map/while/body/eval_jaxpr/reduce_sum | solution.py:93
  154.6 13.1 %fusion.38 = bf16[2,16,64,256]{3,2,1,0:T(8,128)(2,1)S(1)} fusion(f32[2,16,256,1024]{3,2,1,0:T(8,128)} %get-tuple-element.85, f32[2,16,256]{2,1,0:T(8,128)S(1)} %fusion, f32[2,16,256]{2,1,0:T(8,128)S(1)} %get-tuple-element.84, f32[2,1024,16,64]{1,3,2,0:T(8,128)S(1)} %copy-done.4), kind=kOutput, calls=%fused_computation.69 | convolution fusion | flops 1103626240 | bytes 43057152 | tf_op jit(solution)/shard_map/while/body/eval_jaxpr/shqk,skhd->sqhd/dot_general | solution.py:95
  172.5 35.9 %all-gather.3.cloned.1.call-done = bf16[2,1024,1024]{2,1,0:T(8,128)(2,1)} async-done(((bf16[2,256,1024]{2,1,0:T(8,128)(2,1)}), bf16[2,1024,1024]{2,1,0:T(8,128)(2,1)}) %all-gather.3.cloned.1.call-update) | async-done | bytes 4194320 | tf_op jit(solution)/shard_map/all_gather | solution.py:198
  208.4 8.4 fusion.43
  221.8 22.6 %all-gather.5.cloned.1.call-done = bf16[2,1024,1024]{2,1,0:T(8,128)(2,1)} async-done(((bf16[2,256,1024]{2,1,0:T(8,128)(2,1)}), bf16[2,1024,1024]{2,1,0:T(8,128)(2,1)}) %all-gather.5.cloned.1.call-update) | async-done | bytes 4194320 | tf_op jit(solution)/shard_map/all_gather | solution.py:213
  244.4 10.3 %multiply_convert_fusion.3 = (bf16[2,1024,704]{1,2,0:T(8,128)(2,1)S(1)}, bf16[2,1024,704]{1,2,0:T(8,128)(2,1)S(1)}, bf16[2,1024,704]{1,2,0:T(8,128)(2,1)}) fusion(f32[2,1024,704]{1,2,0:T(8,128)} %fusion.47, f32[2,1024,704]{1,2,0:T(8,128)} %fusion.43, bf16[2,1024,1024]{2,1,0:T(8,128)(2,1)} %all-gather.5.cloned.1.call-done, bf16[704,1024]{1,0:T(8,128)(2,1)} %param.18), kind=kOutput, calls=%fused_computation.16 | convolution fusion | flops 2975858688 | bytes 25821184 | tf_op jit(solution)/shard_map/uow,nw->uon/dot_general | solution.py:214
  263.9 7.8 convolution_convert_fusion
  271.8 36.4 %reduce-scatter.6.cloned.1.call-done = bf16[2,256,1024]{2,1,0:T(8,128)(2,1)} async-done(((bf16[2,1024,1024]{2,1,0:T(8,128)(2,1)}), bf16[2,256,1024]{2,1,0:T(8,128)(2,1)}) %reduce-scatter.6.cloned.1.call-update) | async-done | bytes 1048592 | tf_op jit(solution)/shard_map/reduce_scatter | solution.py:227
  311.3 43.8 %reduce-scatter.4.cloned.1.call-done = bf16[2,256,1024]{2,1,0:T(8,128)(2,1)} async-done(((bf16[2,1024,1024]{2,1,0:T(8,128)(2,1)}), bf16[2,256,1024]{2,1,0:T(8,128)(2,1)}) %reduce-scatter.4.cloned.1.call-update) | async-done | bytes 1048592 | tf_op jit(solution)/shard_map/reduce_scatter | solution.py:210
  362.4 25.8 %multiply_reduce_fusion = (f32[2,16,256]{2,1,0:T(8,128)S(1)}, f32[2,16,256,1024]{3,2,1,0:T(8,128)}) fusion(f32[2,16,256,1024]{3,2,1,0:T(8,128)} %get-tuple-element.85, f32[2,16,256]{2,1,0:T(8,128)S(1)} %log_add_fusion, bf16[2,256,16,64]{1,3,2,0:T(8,128)(2,1)S(1)} %bitcast.122, f32[2,1024,16,64]{1,3,2,0:T(8,128)} %copy.89), kind=kOutput, calls=%fused_computation.2 | convolution fusion | flops 1103093760 | bytes 76611584 | tf_op jit(solution)/shard_map/while/body/eval_jaxpr/sqhd,skhd->shqk/dot_general | solution.py:105
  388.2 28.0 %multiply_convert_fusion = bf16[2,16,256,1024]{3,2,1,0:T(8,128)(2,1)} fusion(f32[2,16,256,1024]{3,2,1,0:T(8,128)} %get-tuple-element.89, f32[2,16,256,1024]{3,2,1,0:T(8,128)} %get-tuple-element.85, f32[2,16,256]{2,1,0:T(8,128)S(1)} %get-tuple-element.88, f32[2,16,256]{2,1,0:T(8,128)S(1)} %log_add_fusion), kind=kLoop, calls=%fused_computation.1 | loop fusion | flops 33554432 | bytes 83951616 | tf_op jit(solution)/shard_map/while/body/eval_jaxpr/convert_element_type | solution.py:109
  416.1 12.0 %multiply_bitcast_fusion = f32[2,1024,16,64]{1,3,2,0:T(8,128)} fusion(bf16[2,16,256,1024]{3,2,1,0:T(8,128)(2,1)} %multiply_convert_fusion, f32[2,256,16,64]{1,3,2,0:T(8,128)S(1)} %copy-done.8), kind=kOutput, calls=%fused_computation.12 | convolution fusion | flops 1076887552 | bytes 27262976 | tf_op jit(solution)/shard_map/while/body/eval_jaxpr/shqk,sqhd->skhd/dot_general | solution.py:116
  428.2 14.6 %copy.106 = f32[2,1024,16,64]{3,2,1,0:T(8,128)} copy(f32[2,1024,16,64]{1,3,2,0:T(8,128)} %multiply_bitcast_fusion) | data formatting | bytes 16777216 | tf_op jit(solution)/shard_map/while/body/eval_jaxpr/mul | solution.py:116
  442.8 17.1 %fusion.72 = f32[2,1024,16,2]{2,3,1,0:T(2,128)} fusion(f32[2,1024,16,64]{3,2,1,0:T(8,128)} %copy.106, bf16[2,1024,2,64]{3,2,1,0:T(2,128)(2,1)S(1)} %copy-done.12), kind=kOutput, calls=%fused_computation.126 | convolution fusion | flops 50331648 | bytes 9175040 | tf_op jit(solution)/shard_map/...hd,...rd->...hr/dot_general | solution.py:56
  460.0 9.7 %fusion.73 = f32[2,1024,2,64]{3,2,1,0:T(2,128)} fusion(bf16[2,1024,16,2]{2,3,1,0:T(2,128)(2,1)S(1)} %copy-done.13, f32[2,1024,16,64]{3,2,1,0:T(8,128)S(1)} %copy-done.2), kind=kOutput, calls=%fused_computation.127 | convolution fusion | flops 50331648 | bytes 9568256 | tf_op jit(solution)/shard_map/...hd,...hr->...rd/dot_general | solution.py:59
  469.7 16.8 %fusion.6 = f32[2,1024,16,64]{1,3,2,0:T(8,128)} fusion(bf16[2,256,16,64]{1,3,2,0:T(8,128)(2,1)S(1)} %bitcast.123, f32[2,16,256,1024]{3,2,1,0:T(8,128)} %get-tuple-element.85, f32[2,16,256]{2,1,0:T(8,128)S(1)} %log_add_fusion), kind=kOutput, calls=%fused_computation.27 | convolution fusion | flops 1090519040 | bytes 43024384 | tf_op jit(solution)/shard_map/while/body/eval_jaxpr/shqk,sqhd->skhd/dot_general | solution.py:119
  486.4 14.6 %copy.113 = f32[2,1024,16,64]{3,2,1,0:T(8,128)} copy(f32[2,1024,16,64]{1,3,2,0:T(8,128)} %fusion.6) | data formatting | bytes 16777216 | tf_op jit(solution)/shard_map/while/body/eval_jaxpr/shqk,sqhd->skhd/transpose | solution.py:119
  501.0 17.1 %fusion.74 = f32[2,1024,16,2]{2,3,1,0:T(2,128)} fusion(f32[2,1024,16,64]{3,2,1,0:T(8,128)} %copy.113, bf16[2,1024,2,64]{3,2,1,0:T(2,128)(2,1)S(1)} %copy-done.11), kind=kOutput, calls=%fused_computation.128 | convolution fusion | flops 50331648 | bytes 9175040 | tf_op jit(solution)/shard_map/...hd,...rd->...hr/dot_general | solution.py:56
  518.1 9.9 %fusion.75 = f32[2,1024,2,64]{3,2,1,0:T(2,128)} fusion(bf16[2,1024,16,2]{2,3,1,0:T(2,128)(2,1)S(1)} %copy-done.14, f32[2,1024,16,64]{3,2,1,0:T(8,128)S(1)} %copy-done.3), kind=kOutput, calls=%fused_computation.129 | convolution fusion | flops 50331648 | bytes 9568256 | tf_op jit(solution)/shard_map/...hd,...hr->...rd/dot_general | solution.py:59
  539.1 7.6 bitcast_convert_fusion.1
  555.2 12.4 %multiply_bitcast_fusion.1 = f32[2,256,16,64]{1,3,2,0:T(8,128)} fusion(bf16[2,16,256,1024]{3,2,1,0:T(8,128)(2,1)} %multiply_convert_fusion, f32[2,1024,16,64]{1,3,2,0:T(8,128)} %copy.96), kind=kOutput, calls=%fused_computation.57 | convolution fusion | flops 1078460416 | bytes 27262976 | tf_op jit(solution)/shard_map/while/body/eval_jaxpr/shqk,skhd->sqhd/dot_general | solution.py:112
  572.7 6.9 fusion.71
  596.3 133.1 %all-reduce.8.cloned.1.call-done = (bf16[1024,704]{0,1:T(8,128)(2,1)}, bf16[1024,704]{0,1:T(8,128)(2,1)}, bf16[704,1024]{1,0:T(8,128)(2,1)}) async-done(((bf16[1024,704]{0,1:T(8,128)(2,1)}, bf16[1024,704]{0,1:T(8,128)(2,1)}, bf16[704,1024]{1,0:T(8,128)(2,1)}), (bf16[1024,704]{0,1:T(8,128)(2,1)}, bf16[1024,704]{0,1:T(8,128)(2,1)}, bf16[704,1024]{1,0:T(8,128)(2,1)})) %all-reduce.8.cloned.1.call-update) | async-done | bytes 4325392 | tf_op jit(solution)/shard_map/psum | solution.py:240
  740.5 40.9 %all-reduce = (f32[1024]{0:T(1024)}, f32[1024]{0:T(1024)}) all-reduce(f32[1024]{0:T(1024)S(1)} %get-tuple-element.52, f32[1024]{0:T(1024)S(1)} %copy-done.35), channel_id=1, replica_groups=mesh['rows'=8,'wide'=4] {'rows','wide'}, use_global_device_ids=true, to_apply=%region_13.14 | all-reduce | flops 2048 | bytes 16384 | tf_op jit(solution)/shard_map/psum | solution.py:285
  785.2 120.1 %all-reduce.6.cloned.1.call-done = (f32[1024,800]{0,1:T(8,128)}, f32[1024,1024]{1,0:T(8,128)}) async-done(((f32[1024,800]{0,1:T(8,128)}, f32[1024,1024]{1,0:T(8,128)}), (f32[1024,800]{0,1:T(8,128)}, f32[1024,1024]{1,0:T(8,128)})) %all-reduce.6.cloned.1.call-update) | async-done | bytes 7471120 | tf_op jit(solution)/shard_map/psum | solution.py:285
  (195 shorter events, 139.6 us)
Async XLA Ops:
  7.2 160.6 %copy-start = (bf16[1024,1024]{1,0:T(8,128)(2,1)S(1)}, bf16[1024,1024]{1,0:T(8,128)(2,1)}, u32[]{:S(2)}) copy-start(bf16[1024,1024]{1,0:T(8,128)(2,1)} %param.13) | copy-start | bytes 6291460
  7.2 201.2 %all-gather.3.cloned.1.call-start = ((), (), s32[]{:S(2)}) async-start(), calls=%async_computation.3 | async-start | bytes 5242880 | tf_op jit(solution)/shard_map/all_gather | solution.py:198
  7.2 18.9 %copy-start.41 = (bf16[1024,800]{0,1:T(8,128)(2,1)S(1)}, bf16[1024,800]{0,1:T(8,128)(2,1)}, u32[]{:S(2)}) copy-start(bf16[1024,800]{0,1:T(8,128)(2,1)} %param.12) | copy-start | bytes 4915204
  9.5 34.1 %copy-start.33 = (f32[2,256]{1,0:T(2,128)}, f32[2,256]{1,0:T(2,128)S(1)}, u32[]{:S(2)}) copy-start(f32[2,256]{1,0:T(2,128)S(1)} %get-tuple-element.81) | copy-start | bytes 6148
  11.0 15.1 %copy-start.25 = (bf16[2,256,1024]{2,1,0:T(8,128)(2,1)}, bf16[2,256,1024]{2,1,0:T(8,128)(2,1)S(1)}, u32[]{:S(2)}) copy-start(bf16[2,256,1024]{2,1,0:T(8,128)(2,1)S(1)} %fusion.18) | copy-start | bytes 3145732
  11.1 15.0 %collective-permute-start = (bf16[2,256,1024]{2,1,0:T(8,128)(2,1)S(1)}, bf16[2,256,1024]{2,1,0:T(8,128)(2,1)}, u32[]{:S(2)}, u32[]{:S(2)}) collective-permute-start(bf16[2,256,1024]{2,1,0:T(8,128)(2,1)S(1)} %fusion.18), channel_id=1, source_target_pairs={{0,1},{1,2},{2,3},{3,0},{4,5},{5,6},{6,7},{7,4},{8,9},{9,10},{10,1... | collective-permute-start | bytes 3145736 | tf_op jit(solution)/shard_map/ppermute | solution.py:32
  26.1 14.5 %collective-permute-start.1 = (bf16[2,256,1024]{2,1,0:T(8,128)(2,1)}, bf16[2,256,1024]{2,1,0:T(8,128)(2,1)}, u32[]{:S(2)}, u32[]{:S(2)}) collective-permute-start(bf16[2,256,1024]{2,1,0:T(8,128)(2,1)} %collective-permute-done), channel_id=1, source_target_pairs={{0,1},{1,2},{2,3},{3,0},{4,5},{5,6},{6,7},{7,4},{8,9},{9,10},{10,1... | collective-permute-start | bytes 3145736 | tf_op jit(solution)/shard_map/ppermute | solution.py:32
  34.8 8.8 copy-start.6
  34.8 8.8 copy-start.31
  40.6 14.6 %collective-permute-start.2 = (bf16[2,256,1024]{2,1,0:T(8,128)(2,1)}, bf16[2,256,1024]{2,1,0:T(8,128)(2,1)S(1)}, u32[]{:S(2)}, u32[]{:S(2)}) collective-permute-start(bf16[2,256,1024]{2,1,0:T(8,128)(2,1)} %collective-permute-done.1), channel_id=1, source_target_pairs={{0,1},{1,2},{2,3},{3,0},{4,5},{5,6},{6,7},{7,4},{8,9},{9,10},{10,1... | collective-permute-start | bytes 3145736 | tf_op jit(solution)/shard_map/ppermute | solution.py:32
  139.9 14.7 %copy-start.4 = (f32[2,1024,16,64]{1,3,2,0:T(8,128)S(1)}, f32[2,1024,16,64]{1,3,2,0:T(8,128)}, u32[]{:S(2)}) copy-start(f32[2,1024,16,64]{1,3,2,0:T(8,128)} %copy.89) | copy-start | bytes 25165828
  171.7 72.7 %all-gather.5.cloned.1.call-start = ((), (), s32[]{:S(2)}) async-start(), calls=%async_computation.5 | async-start | bytes 5242880 | tf_op jit(solution)/shard_map/all_gather | solution.py:213
  172.5 135.7 %reduce-scatter.6.cloned.1.call-start = ((), (), s32[]{:S(2)}) async-start(), calls=%async_computation.6 | async-start | bytes 5242880 | tf_op jit(solution)/shard_map/reduce_scatter | solution.py:227
  208.4 8.4 copy-start.38
  208.4 8.4 copy-start.43
  244.4 10.4 %copy-start.44 = (bf16[1024,704]{0,1:T(8,128)(2,1)S(1)}, bf16[1024,704]{0,1:T(8,128)(2,1)}, u32[]{:S(2)}) copy-start(bf16[1024,704]{0,1:T(8,128)(2,1)} %param.16) | copy-start | bytes 4325380
  263.4 91.7 %reduce-scatter.4.cloned.1.call-start = ((), (), s32[]{:S(2)}) async-start(), calls=%async_computation.4 | async-start | bytes 5242880 | tf_op jit(solution)/shard_map/reduce_scatter | solution.py:210
  271.7 83.5 %copy-start.22 = (bf16[2,256,1024]{2,1,0:T(8,128)(2,1)S(1)}, bf16[2,256,1024]{2,1,0:T(8,128)(2,1)}, u32[]{:S(2)}) copy-start(bf16[2,256,1024]{2,1,0:T(8,128)(2,1)} %param.19) | copy-start | bytes 3145732
  271.7 320.8 %reduce-scatter.8.cloned.1.call-start = ((), (), s32[]{:S(2)}) async-start(), calls=%async_computation.7 | async-start | bytes 1638400 | tf_op jit(solution)/shard_map/reduce_scatter | solution.py:273
  362.3 25.8 %copy-start.9 = (bf16[2,256,1024]{1,2,0:T(8,128)(2,1)}, bf16[2,256,1024]{1,2,0:T(8,128)(2,1)S(1)}, u32[]{:S(2)}) copy-start(bf16[2,256,1024]{1,2,0:T(8,128)(2,1)S(1)} %copy.98) | copy-start | bytes 3145732
  388.2 28.0 %copy-start.8 = (f32[2,256,16,64]{1,3,2,0:T(8,128)S(1)}, f32[2,256,16,64]{1,3,2,0:T(8,128)}, u32[]{:S(2)}) copy-start(f32[2,256,16,64]{1,3,2,0:T(8,128)} %copy.93) | copy-start | bytes 6291460
  428.2 14.7 %copy-start.12 = (bf16[2,1024,2,64]{3,2,1,0:T(2,128)(2,1)S(1)}, bf16[2,1024,2,64]{3,2,1,0:T(2,128)(2,1)}, u32[]{:S(2)}) copy-start(bf16[2,1024,2,64]{3,2,1,0:T(2,128)(2,1)} %copy.95) | copy-start | bytes 1572868
  442.8 17.2 %copy-start.2 = (f32[2,1024,16,64]{3,2,1,0:T(8,128)S(1)}, f32[2,1024,16,64]{3,2,1,0:T(8,128)}, u32[]{:S(2)}) copy-start(f32[2,1024,16,64]{3,2,1,0:T(8,128)} %copy.106) | copy-start | bytes 25165828
  442.8 17.2 %copy-start.13 = (bf16[2,1024,16,2]{2,3,1,0:T(2,128)(2,1)S(1)}, bf16[2,1024,16,2]{2,3,1,0:T(2,128)(2,1)}, u32[]{:S(2)}) copy-start(bf16[2,1024,16,2]{2,3,1,0:T(2,128)(2,1)} %copy.94) | copy-start | bytes 393220
  460.0 9.7 %copy-start.10 = (bf16[2,256,1024]{1,2,0:T(8,128)(2,1)S(1)}, bf16[2,256,1024]{1,2,0:T(8,128)(2,1)}, u32[]{:S(2)}) copy-start(bf16[2,256,1024]{1,2,0:T(8,128)(2,1)} %copy-done.9) | copy-start | bytes 3145732
  486.4 14.6 %copy-start.11 = (bf16[2,1024,2,64]{3,2,1,0:T(2,128)(2,1)S(1)}, bf16[2,1024,2,64]{3,2,1,0:T(2,128)(2,1)}, u32[]{:S(2)}) copy-start(bf16[2,1024,2,64]{3,2,1,0:T(2,128)(2,1)} %copy.88) | copy-start | bytes 1572868
  501.0 17.1 %copy-start.3 = (f32[2,1024,16,64]{3,2,1,0:T(8,128)S(1)}, f32[2,1024,16,64]{3,2,1,0:T(8,128)}, u32[]{:S(2)}) copy-start(f32[2,1024,16,64]{3,2,1,0:T(8,128)} %copy.113) | copy-start | bytes 25165828
  501.0 17.1 %copy-start.14 = (bf16[2,1024,16,2]{2,3,1,0:T(2,128)(2,1)S(1)}, bf16[2,1024,16,2]{2,3,1,0:T(2,128)(2,1)}, u32[]{:S(2)}) copy-start(bf16[2,1024,16,2]{2,3,1,0:T(2,128)(2,1)} %copy.87) | copy-start | bytes 393220
  539.0 190.4 %all-reduce.8.cloned.1.call-start = ((), (), s32[]{:S(2)}) async-start(), calls=%async_computation.9 | async-start | bytes 8650752 | tf_op jit(solution)/shard_map/psum | solution.py:240
  539.0 7.6 copy-start.39
  555.1 350.2 %all-reduce.6.cloned.1.call-start = ((), (), s32[]{:S(2)}) async-start(), calls=%async_computation.8 | async-start | bytes 14942208 | tf_op jit(solution)/shard_map/psum | solution.py:285
  737.6 43.8 %copy-start.37 = (f32[2,256]{1,0:T(2,128)S(1)}, f32[2,256]{1,0:T(2,128)}, u32[]{:S(2)}) copy-start(f32[2,256]{1,0:T(2,128)} %get-tuple-element.80) | copy-start | bytes 6148
  (29 other events, 103.4 us)
Sparse Core Ops, SparseCore 0:
  171.8 36.4 all-gather.2
  209.9 34.4 all-gather.4
  263.6 44.5 reduce-scatter.5
  310.5 44.5 reduce-scatter.3
  539.1 26.4 reduce-scatter.7
  569.9 159.4 all-reduce.7
  736.0 169.1 all-reduce.5
